TPU v7x, 32 devices: a whole 2x2x4 slice. The times are simulated.
32 devices in a mesh: dp: 2 (over y), expert: 16 (over z, x, core).
Axes of the slice: x: 2, y: 2, z: 4, core: 2. Of those that a mesh axis runs over, the one named last changes fastest.
Arguments:
- tokens: bfloat16 [2048, 3584], P('expert', 'dp'), may hold values from -6 to 6
- expert_ids: int32 [2048, 8], P('expert'), may hold values from 0 to 63, all different within a row; in each aligned block of 128 rows (0 to 127, 128 to 255, ...) at most 32 rows name the same one
- gate_weight: float32 [2048, 8], P('expert'), may hold values from 0.1 to 0.6
- w_gate: bfloat16 [16, 3584, 1024], P('expert', 'dp'), may hold values from -0.09375 to 0.09375
- w_up: bfloat16 [16, 3584, 1024], P('expert', 'dp'), may hold values from -0.09375 to 0.09375
- w_down: bfloat16 [16, 1024, 3584], P('expert', None, 'dp'), may hold values from -0.1875 to 0.1875
- grad_out: bfloat16 [2048, 3584], P('expert', 'dp'), may hold values from -6 to 6
Outputs:
- output: bfloat16 [2048, 3584], P('expert', 'dp')
- grad_tokens: bfloat16 [2048, 3584], P('expert', 'dp')
- grad_down: bfloat16 [16, 1024, 3584], P('expert', None, 'dp')
Inputs may be any that keep to these rules, and one draw needn't show every extreme that they name: `expert_ids`: each row names 8 different experts. Among the rows of one device no expert is named by more than 32 rows, and in some device's rows some expert is named by exactly 32 rows.
All inputs are finite; a program needn't handle non-finite values.
Results may differ from a plain program's by a relative error of at most 0.024.
Values may be sent and summed in bfloat16 or wider, within the bound.
A program may use at most 64 MiB of HBM per device.

v0:
```python
import jax
import jax.numpy as jnp
from jax import lax
from jax.sharding import PartitionSpec as P


def dp_sum(part):
    count = lax.axis_size("dp")
    part = part.astype(jnp.bfloat16)
    total = part.astype(jnp.float32)
    for shift in range(1, count):
        moved = lax.ppermute(part, "dp", [(i, (i + shift) % count) for i in range(count)])
        total = total + moved.astype(jnp.float32)
    return total


def local(tokens, expert_ids, gate_weight, w_gate, w_up, w_down, grad_out):
    tok_dev, fanout = expert_ids.shape
    feature_cols = tokens.shape[1]
    experts = lax.axis_size("expert")
    capacity = max(2, min(tok_dev, 2 * tok_dev * fanout // (4 * experts)))
    ids = jnp.arange(experts, dtype=jnp.int32)
    named = expert_ids[None, :, :] == ids[:, None, None]
    hot = jnp.any(named, axis=2)
    gate_of = jnp.sum(jnp.where(named, gate_weight[None, :, :], 0.0), axis=2)
    rows = jnp.arange(tok_dev, dtype=jnp.int32)
    earlier = (rows[:, None] < rows[None, :]).astype(jnp.bfloat16)
    before = jnp.dot(hot.astype(jnp.bfloat16), earlier, preferred_element_type=jnp.float32)
    slot_of = jnp.where(hot, before.astype(jnp.int32), -1)
    placing = slot_of[:, None, :] == jnp.arange(capacity, dtype=jnp.int32)[None, :, None]
    select = placing.astype(jnp.bfloat16).reshape(experts * capacity, tok_dev)
    slot_gate = jnp.sum(jnp.where(placing, gate_of[:, None, :], 0.0), axis=2).reshape(
        experts * capacity
    )
    x_slab = jnp.dot(select, tokens, preferred_element_type=jnp.float32).astype(jnp.bfloat16)
    x_slab = x_slab.reshape(experts, capacity, feature_cols)
    cot_rows = jnp.dot(select, grad_out, preferred_element_type=jnp.float32)
    c_slab = (slot_gate[:, None] * cot_rows).astype(jnp.bfloat16)
    c_slab = c_slab.reshape(experts, capacity, feature_cols)
    gate_mat = w_gate[0]
    up_mat = w_up[0]
    down_mat = w_down[0]
    row_total = experts * capacity
    transposed = (((1,), (1,)), ((), ()))
    arrived = lax.all_to_all(x_slab, "expert", split_axis=0, concat_axis=0, tiled=True)
    x_rows = arrived.reshape(row_total, feature_cols)
    gate_part = jnp.dot(x_rows, gate_mat, preferred_element_type=jnp.float32)
    up_part = jnp.dot(x_rows, up_mat, preferred_element_type=jnp.float32)
    gate_pre = dp_sum(gate_part)
    up_pre = dp_sum(up_part)
    hidden = (jax.nn.silu(gate_pre) * up_pre).astype(jnp.bfloat16)
    out_rows = jnp.dot(hidden, down_mat, preferred_element_type=jnp.float32).astype(jnp.bfloat16)
    gate_pre, up_pre, hidden, out_rows = (
        gate_pre,
        up_pre,
        hidden,
        out_rows.reshape(experts, capacity, feature_cols),
    )
    back_out = lax.all_to_all(out_rows, "expert", split_axis=0, concat_axis=0, tiled=True)
    arrived_grads = lax.all_to_all(c_slab, "expert", split_axis=0, concat_axis=0, tiled=True)
    c_rows = arrived_grads.reshape(row_total, feature_cols)
    hidden_part = lax.dot_general(c_rows, down_mat, transposed, preferred_element_type=jnp.float32)
    sig = jax.nn.sigmoid(gate_pre)
    grad_hidden = dp_sum(hidden_part)
    grad_gate = (grad_hidden * up_pre * sig * (1.0 + gate_pre * (1.0 - sig))).astype(jnp.bfloat16)
    grad_up = (grad_hidden * jax.nn.silu(gate_pre)).astype(jnp.bfloat16)
    grad_rows = lax.dot_general(grad_gate, gate_mat, transposed, preferred_element_type=jnp.float32)
    grad_rows = grad_rows + lax.dot_general(
        grad_up, up_mat, transposed, preferred_element_type=jnp.float32
    )
    grad_rows = grad_rows.astype(jnp.bfloat16).reshape(experts, capacity, feature_cols)
    down_grad = lax.dot_general(
        hidden, c_rows, (((0,), (0,)), ((), ())), preferred_element_type=jnp.float32
    )
    grad_rows, down_grad = (grad_rows, down_grad.astype(jnp.bfloat16))
    back_grads = lax.all_to_all(grad_rows, "expert", split_axis=0, concat_axis=0, tiled=True)
    scaled = back_out.reshape(row_total, feature_cols).astype(jnp.float32) * slot_gate[:, None]
    output = jnp.dot(select.T, scaled.astype(jnp.bfloat16), preferred_element_type=jnp.float32)
    output = output.astype(jnp.bfloat16)
    grad_flat = back_grads.reshape(row_total, feature_cols)
    grad_tokens = jnp.dot(select.T, grad_flat, preferred_element_type=jnp.float32).astype(
        jnp.bfloat16
    )
    return (output, grad_tokens, down_grad.reshape(1, down_grad.shape[0], feature_cols))


def solution(mesh):
    return jax.shard_map(
        local,
        mesh=mesh,
        in_specs=(
            P("expert", "dp"),
            P("expert", None),
            P("expert", None),
            P("expert", "dp", None),
            P("expert", "dp", None),
            P("expert", None, "dp"),
            P("expert", "dp"),
        ),
        out_specs=(P("expert", "dp"), P("expert", "dp"), P("expert", None, "dp")),
        check_vma=False,
    )
```

profile of v0, /device:TPU:15, one launch (start us, length us, event | category | flops | bytes accessed | tf_op | source)
XLA Modules:
  0.0 262.5 jit_solution(12682456211212196916)
XLA Ops:
  0.6 0.8 fusion.36
  1.4 0.1 fusion.31
  1.6 0.7 select_reduce_fusion.1
  2.3 0.1 select_reduce_fusion
  2.5 0.1 eq.46
  2.6 0.1 bitcast_compare_fusion
  2.8 1.9 multiply_convert_fusion
  4.7 6.7 %all-to-all-start.2 = ((bf16[16,32,1792]{2,1,0:T(8,128)(2,1)}), bf16[16,32,1792]{2,1,0:T(8,128)(2,1)S(1)}, u32[]{:S(2)}, u32[]{:S(2)}) async-start(bf16[16,32,1792]{2,1,0:T(8,128)(2,1)} %bitcast.8), calls=%async_computation.2 | async-start | bytes 3670016 | tf_op jit(solution)/shard_map/all_to_all | solution.py:60
  11.3 1.9 convolution_convert_fusion.1
  13.2 39.9 %all-to-all-done.2 = bf16[16,32,1792]{2,1,0:T(8,128)(2,1)S(1)} async-done(((bf16[16,32,1792]{2,1,0:T(8,128)(2,1)}), bf16[16,32,1792]{2,1,0:T(8,128)(2,1)S(1)}, u32[]{:S(2)}, u32[]{:S(2)}) %all-to-all-start.2) | async-done | bytes 1835040 | tf_op jit(solution)/shard_map/all_to_all | solution.py:60
  53.1 4.8 %all-to-all-start = ((bf16[16,32,1792]{2,1,0:T(8,128)(2,1)}), bf16[16,32,1792]{2,1,0:T(8,128)(2,1)}, u32[]{:S(2)}, u32[]{:S(2)}) async-start(bf16[16,32,1792]{2,1,0:T(8,128)(2,1)} %bitcast.1), calls=%async_computation | async-start | bytes 3670016 | tf_op jit(solution)/shard_map/all_to_all | solution.py:45
  57.9 4.1 %fusion.28 = bf16[512,1024]{1,0:T(8,128)(2,1)S(1)} fusion(bf16[512,1792]{1,0:T(8,128)(2,1)S(1)} %bitcast.55, bf16[1,1024,1792]{2,1,0:T(8,128)(2,1)} %param.12), kind=kOutput, calls=%fused_computation.34 | convolution fusion | flops 1879572480 | bytes 6553600 | tf_op jit(solution)/shard_map/dot_general | solution.py:62
  62.0 0.3 collective-permute-start.2
  62.3 37.5 %all-to-all-done = bf16[16,32,1792]{2,1,0:T(8,128)(2,1)} async-done(((bf16[16,32,1792]{2,1,0:T(8,128)(2,1)}), bf16[16,32,1792]{2,1,0:T(8,128)(2,1)}, u32[]{:S(2)}, u32[]{:S(2)}) %all-to-all-start) | async-done | bytes 1835040 | tf_op jit(solution)/shard_map/all_to_all | solution.py:45
  99.8 4.8 %fusion.22 = bf16[512,1024]{1,0:T(8,128)(2,1)S(1)} fusion(bf16[512,1792]{1,0:T(8,128)(2,1)} %bitcast.2, bf16[1,1792,1024]{2,1,0:T(8,128)(2,1)} %param.10), kind=kOutput, calls=%fused_computation.32 | convolution fusion | flops 1879572480 | bytes 6553600 | tf_op jit(solution)/shard_map/dot_general | solution.py:47
  104.6 3.7 %fusion.25 = bf16[512,1024]{1,0:T(8,128)(2,1)S(1)} fusion(bf16[512,1792]{1,0:T(8,128)(2,1)} %bitcast.2, bf16[1,1792,1024]{2,1,0:T(8,128)(2,1)S(1)} %copy-done.9), kind=kOutput, calls=%fused_computation.33 | convolution fusion | flops 1879572480 | bytes 6553600 | tf_op jit(solution)/shard_map/dot_general | solution.py:48
  108.4 0.3 collective-permute-start.1
  108.7 1.2 collective-permute-start
  109.9 23.1 %collective-permute-done.1 = bf16[512,1024]{1,0:T(8,128)(2,1)S(1)} collective-permute-done((bf16[512,1024]{1,0:T(8,128)(2,1)S(1)}, bf16[512,1024]{1,0:T(8,128)(2,1)S(1)}, u32[]{:S(2)}, u32[]{:S(2)}) %collective-permute-start.1) | collective-permute-done | bytes 1048608 | tf_op jit(solution)/shard_map/ppermute | solution.py:12
  133.1 22.5 %collective-permute-done = bf16[512,1024]{1,0:T(8,128)(2,1)S(1)} collective-permute-done((bf16[512,1024]{1,0:T(8,128)(2,1)S(1)}, bf16[512,1024]{1,0:T(8,128)(2,1)S(1)}, u32[]{:S(2)}, u32[]{:S(2)}) %collective-permute-start) | collective-permute-done | bytes 1048608 | tf_op jit(solution)/shard_map/ppermute | solution.py:12
  155.6 4.8 %fusion.8 = f32[512,1792]{1,0:T(8,128)S(1)} fusion(bf16[1,1792,1024]{2,1,0:T(8,128)(2,1)S(1)} %copy-done.8, bf16[512,1024]{1,0:T(8,128)(2,1)S(1)} %collective-permute-done, bf16[512,1024]{1,0:T(8,128)(2,1)S(1)} %fusion.22, bf16[512,1024]{1,0:T(8,128)(2,1)S(1)} %collective-permute-done.1, bf16[512,1024]{1,0:T(8,128)(2,1)S(1)} %fusion.25, ...), kind=kOutput, calls=%fused_computation.9 | convolution fusion | flops 1889009664 | bytes 13631488 | tf_op jit(solution)/shard_map/dot_general | solution.py:67
  160.4 5.2 %add_convert_fusion = bf16[512,1792]{1,0:T(8,128)(2,1)} fusion(f32[512,1792]{1,0:T(8,128)S(1)} %fusion.8, bf16[1,1792,1024]{2,1,0:T(8,128)(2,1)S(1)} %copy-done.9, bf16[512,1024]{1,0:T(8,128)(2,1)} %collective-permute-done.2, bf16[512,1024]{1,0:T(8,128)(2,1)S(1)} %fusion.28, bf16[512,1024]{1,0:T(8,128)(2,1)S(1)} %collective-permute-done, ...), kind=kOutput, calls=%fused_computation.13 | convolution fusion | flops 1887174656 | bytes 13369344 | tf_op jit(solution)/shard_map/dot_general | solution.py:68
  165.6 5.6 %all-to-all-start.3 = ((bf16[16,32,1792]{2,1,0:T(8,128)(2,1)}), bf16[16,32,1792]{2,1,0:T(8,128)(2,1)S(1)}, u32[]{:S(2)}, u32[]{:S(2)}) async-start(bf16[16,32,1792]{2,1,0:T(8,128)(2,1)} %bitcast.58), calls=%async_computation.3 | async-start | bytes 3670016 | tf_op jit(solution)/shard_map/all_to_all | solution.py:76
  171.2 3.0 %multiply_convert_fusion.4 = bf16[512,1024]{1,0:T(8,128)(2,1)S(1)} fusion(bf16[512,1024]{1,0:T(8,128)(2,1)} %copy-done.3, bf16[512,1024]{1,0:T(8,128)(2,1)} %copy-done.2, bf16[512,1024]{1,0:T(8,128)(2,1)} %copy-done.4, bf16[512,1024]{1,0:T(8,128)(2,1)S(1)} %fusion.22), kind=kLoop, calls=%fused_computation.26 | loop fusion | flops 6291456 | bytes 5242880 | tf_op jit(solution)/shard_map/convert_element_type | solution.py:51
  174.3 1.0 copy-done.5
  175.2 3.3 %fusion.15 = bf16[512,1792]{1,0:T(8,128)(2,1)} fusion(bf16[512,1024]{1,0:T(8,128)(2,1)S(1)} %multiply_convert_fusion.4, bf16[1,1024,1792]{2,1,0:T(8,128)(2,1)S(1)} %copy-done.10), kind=kOutput, calls=%fused_computation.17 | convolution fusion | flops 1879965696 | bytes 6553600 | tf_op jit(solution)/shard_map/dot_general | solution.py:52
  178.6 34.4 %all-to-all-done.3 = bf16[16,32,1792]{2,1,0:T(8,128)(2,1)S(1)} async-done(((bf16[16,32,1792]{2,1,0:T(8,128)(2,1)}), bf16[16,32,1792]{2,1,0:T(8,128)(2,1)S(1)}, u32[]{:S(2)}, u32[]{:S(2)}) %all-to-all-start.3) | async-done | bytes 1835040 | tf_op jit(solution)/shard_map/all_to_all | solution.py:76
  213.0 4.8 %all-to-all-start.1 = ((bf16[16,32,1792]{2,1,0:T(8,128)(2,1)}), bf16[16,32,1792]{2,1,0:T(8,128)(2,1)}, u32[]{:S(2)}, u32[]{:S(2)}) async-start(bf16[16,32,1792]{2,1,0:T(8,128)(2,1)} %bitcast.57), calls=%async_computation.1 | async-start | bytes 3670016 | tf_op jit(solution)/shard_map/all_to_all | solution.py:59
  217.8 5.5 %fusion.12 = bf16[1,1024,1792]{2,1,0:T(8,128)(2,1)} fusion(bf16[512,1024]{1,0:T(8,128)(2,1)S(1)} %copy-done.6, bf16[512,1792]{1,0:T(8,128)(2,1)} %bitcast.56), kind=kOutput, calls=%fused_computation.16 | convolution fusion | flops 1880883200 | bytes 6553600 | tf_op jit(solution)/shard_map/dot_general | solution.py:72
  223.2 1.2 fusion.19
  224.4 35.2 %all-to-all-done.1 = bf16[16,32,1792]{2,1,0:T(8,128)(2,1)} async-done(((bf16[16,32,1792]{2,1,0:T(8,128)(2,1)}), bf16[16,32,1792]{2,1,0:T(8,128)(2,1)}, u32[]{:S(2)}, u32[]{:S(2)}) %all-to-all-start.1) | async-done | bytes 1835040 | tf_op jit(solution)/shard_map/all_to_all | solution.py:59
  259.7 2.8 %fusion.18 = bf16[128,1792]{1,0:T(8,128)(2,1)} fusion(bf16[16,32,1792]{2,1,0:T(8,128)(2,1)} %all-to-all-done.1, f32[16,32]{1,0:T(8,128)S(1)} %select_reduce_fusion, s32[16,128]{1,0:T(8,128)S(1)} %fusion.31), kind=kOutput, calls=%fused_computation.21 | convolution fusion | flops 237928448 | bytes 2304000 | tf_op jit(solution)/shard_map/dot_general | solution.py:78
  (24 shorter events, 0.1 us)
Async XLA Ops:
  0.6 2.1 copy-start
  4.7 6.7 %copy-start.7 = (bf16[128,1792]{1,0:T(8,128)(2,1)S(1)}, bf16[128,1792]{1,0:T(8,128)(2,1)}, u32[]{:S(2)}) copy-start(bf16[128,1792]{1,0:T(8,128)(2,1)} %param.7) | copy-start | bytes 1376260
  4.7 48.5 %all-to-all-start.2 = ((bf16[16,32,1792]{2,1,0:T(8,128)(2,1)}), bf16[16,32,1792]{2,1,0:T(8,128)(2,1)S(1)}, u32[]{:S(2)}, u32[]{:S(2)}) async-start(bf16[16,32,1792]{2,1,0:T(8,128)(2,1)} %bitcast.8), calls=%async_computation.2 | async-start | bytes 3670016 | tf_op jit(solution)/shard_map/all_to_all | solution.py:60
  53.1 8.9 %copy-start.1 = (bf16[16,32,1792]{2,1,0:T(8,128)(2,1)}, bf16[16,32,1792]{2,1,0:T(8,128)(2,1)S(1)}, u32[]{:S(2)}) copy-start(bf16[16,32,1792]{2,1,0:T(8,128)(2,1)S(1)} %all-to-all-done.2) | copy-start | bytes 5505028
  53.1 46.7 %all-to-all-start = ((bf16[16,32,1792]{2,1,0:T(8,128)(2,1)}), bf16[16,32,1792]{2,1,0:T(8,128)(2,1)}, u32[]{:S(2)}, u32[]{:S(2)}) async-start(bf16[16,32,1792]{2,1,0:T(8,128)(2,1)} %bitcast.1), calls=%async_computation | async-start | bytes 3670016 | tf_op jit(solution)/shard_map/all_to_all | solution.py:45
  62.0 47.9 %collective-permute-start.2 = (bf16[512,1024]{1,0:T(8,128)(2,1)S(1)}, bf16[512,1024]{1,0:T(8,128)(2,1)}, u32[]{:S(2)}, u32[]{:S(2)}) collective-permute-start(bf16[512,1024]{1,0:T(8,128)(2,1)S(1)} %fusion.28), channel_id=1, source_target_pairs={{0,16},{16,0},{1,17},{17,1},{2,18},{18,2},{3,19},{19,3},{4,20},{20... | collective-permute-start | bytes 3145736 | tf_op jit(solution)/shard_map/ppermute | solution.py:12
  99.8 4.8 %copy-start.9 = (bf16[1,1792,1024]{2,1,0:T(8,128)(2,1)S(1)}, bf16[1,1792,1024]{2,1,0:T(8,128)(2,1)}, u32[]{:S(2)}) copy-start(bf16[1,1792,1024]{2,1,0:T(8,128)(2,1)} %param.11) | copy-start | bytes 11010052
  104.6 50.9 %copy-start.8 = (bf16[1,1792,1024]{2,1,0:T(8,128)(2,1)S(1)}, bf16[1,1792,1024]{2,1,0:T(8,128)(2,1)}, u32[]{:S(2)}) copy-start(bf16[1,1792,1024]{2,1,0:T(8,128)(2,1)} %param.10) | copy-start | bytes 11010052
  108.4 47.2 %copy-start.2 = (bf16[512,1024]{1,0:T(8,128)(2,1)}, bf16[512,1024]{1,0:T(8,128)(2,1)S(1)}, u32[]{:S(2)}) copy-start(bf16[512,1024]{1,0:T(8,128)(2,1)S(1)} %fusion.25) | copy-start | bytes 3145732
  108.4 24.7 %collective-permute-start.1 = (bf16[512,1024]{1,0:T(8,128)(2,1)S(1)}, bf16[512,1024]{1,0:T(8,128)(2,1)S(1)}, u32[]{:S(2)}, u32[]{:S(2)}) collective-permute-start(bf16[512,1024]{1,0:T(8,128)(2,1)S(1)} %fusion.25), channel_id=1, source_target_pairs={{0,16},{16,0},{1,17},{17,1},{2,18},{18,2},{3,19},{19,3},{4,20},{20... | collective-permute-start | bytes 3145736 | tf_op jit(solution)/shard_map/ppermute | solution.py:12
  108.7 46.9 %collective-permute-start = (bf16[512,1024]{1,0:T(8,128)(2,1)S(1)}, bf16[512,1024]{1,0:T(8,128)(2,1)S(1)}, u32[]{:S(2)}, u32[]{:S(2)}) collective-permute-start(bf16[512,1024]{1,0:T(8,128)(2,1)S(1)} %fusion.22), channel_id=1, source_target_pairs={{0,16},{16,0},{1,17},{17,1},{2,18},{18,2},{3,19},{19,3},{4,20},{20... | collective-permute-start | bytes 3145736 | tf_op jit(solution)/shard_map/ppermute | solution.py:12
  133.1 22.5 %copy-start.3 = (bf16[512,1024]{1,0:T(8,128)(2,1)}, bf16[512,1024]{1,0:T(8,128)(2,1)S(1)}, u32[]{:S(2)}) copy-start(bf16[512,1024]{1,0:T(8,128)(2,1)S(1)} %collective-permute-done.1) | copy-start | bytes 3145732
  155.5 4.8 %copy-start.4 = (bf16[512,1024]{1,0:T(8,128)(2,1)}, bf16[512,1024]{1,0:T(8,128)(2,1)S(1)}, u32[]{:S(2)}) copy-start(bf16[512,1024]{1,0:T(8,128)(2,1)S(1)} %collective-permute-done) | copy-start | bytes 3145732
  165.6 47.4 %all-to-all-start.3 = ((bf16[16,32,1792]{2,1,0:T(8,128)(2,1)}), bf16[16,32,1792]{2,1,0:T(8,128)(2,1)S(1)}, u32[]{:S(2)}, u32[]{:S(2)}) async-start(bf16[16,32,1792]{2,1,0:T(8,128)(2,1)} %bitcast.58), calls=%async_computation.3 | async-start | bytes 3670016 | tf_op jit(solution)/shard_map/all_to_all | solution.py:76
  171.2 4.0 %copy-start.10 = (bf16[1,1024,1792]{2,1,0:T(8,128)(2,1)S(1)}, bf16[1,1024,1792]{2,1,0:T(8,128)(2,1)}, u32[]{:S(2)}) copy-start(bf16[1,1024,1792]{2,1,0:T(8,128)(2,1)} %param.12) | copy-start | bytes 11010052
  174.2 1.0 copy-start.5
  178.6 39.2 %copy-start.6 = (bf16[512,1024]{1,0:T(8,128)(2,1)S(1)}, bf16[512,1024]{1,0:T(8,128)(2,1)}, u32[]{:S(2)}) copy-start(bf16[512,1024]{1,0:T(8,128)(2,1)} %copy-done.5) | copy-start | bytes 3145732
  213.0 46.7 %all-to-all-start.1 = ((bf16[16,32,1792]{2,1,0:T(8,128)(2,1)}), bf16[16,32,1792]{2,1,0:T(8,128)(2,1)}, u32[]{:S(2)}, u32[]{:S(2)}) async-start(bf16[16,32,1792]{2,1,0:T(8,128)(2,1)} %bitcast.57), calls=%async_computation.1 | async-start | bytes 3670016 | tf_op jit(solution)/shard_map/all_to_all | solution.py:59
where the time goes:
time: 263 us
  waiting for transfers between devices  193 us (73%)
  matrix products  39.4 us (15%)
  starting transfers between devices  23.7 us (9%)
  other arithmetic  4.83 us (2%)
    ppermute x3, waiting for transfers between devices, dp_sum(): lax.ppermute(part, 'dp', [(i, (i + shift) % count) for i in range(count)])  45.6 us
    all_to_all x1, waiting for transfers between devices, local(): lax.all_to_all(c_slab, 'expert', split_axis=0, concat_axis=0, tiled=True)  39.9 us
    all_to_all x1, waiting for transfers between devices, local(): lax.all_to_all(x_slab, 'expert', split_axis=0, concat_axis=0, tiled=True)  37.5 us
    all_to_all x1, waiting for transfers between devices, local(): lax.all_to_all(out_rows, 'expert', split_axis=0, concat_axis=0, tiled=True)  35.2 us
    all_to_all x1, waiting for transfers between devices, local(): lax.all_to_all(grad_rows, 'expert', split_axis=0, concat_axis=0, tiled=True)  34.4 us
    all_to_all x1, starting transfers between devices, local(): lax.all_to_all(c_slab, 'expert', split_axis=0, concat_axis=0, tiled=True)  6.65 us
    all_to_all x1, starting transfers between devices, local(): lax.all_to_all(grad_rows, 'expert', split_axis=0, concat_axis=0, tiled=True)  5.63 us
    dot_general x1, matrix products, local(): lax.dot_general(hidden, c_rows, (((0,), (0,)), ((), ())), preferred_eleme...  5.45 us
  transfers between devices with their start and end apart: 7, of which 6 were waited for; matrix products, arithmetic and copies ran while one was open for 11% of the time, Pallas kernels for 0%

commit v1 on v0

--- a/solution.py
+++ b/solution.py
@@ -2,6 +2,18 @@
 import jax.numpy as jnp
 from jax import lax
 from jax.sharding import PartitionSpec as P
+
+
+def _guide_point(frame_in, d0, work_x):
+    r_now = frame_in.shape
+    met_up = frame_in.reshape(*r_now[:d0], work_x, r_now[d0] // work_x, *r_now[d0 + 1 :])
+    return jnp.moveaxis(met_up, d0, 0)
+
+
+def _treat_keys(buf, axis_k):
+    base_arr = list(buf.shape[1:])
+    base_arr[axis_k] *= buf.shape[0]
+    return jnp.moveaxis(buf, 0, axis_k).reshape(base_arr)
 
 
 def dp_sum(part):
@@ -42,7 +54,28 @@
     down_mat = w_down[0]
     row_total = experts * capacity
     transposed = (((1,), (1,)), ((), ()))
-    arrived = lax.all_to_all(x_slab, "expert", split_axis=0, concat_axis=0, tiled=True)
+
+    def read_sheet_on(raw, lane_axis, mine_x, slab_in):
+        step_out = lax.axis_size(lane_axis)
+        current_arr = lax.axis_index(lane_axis)
+        response, local_out = (step_out, current_arr)
+        back = _guide_point(raw, mine_x, response)
+        xs_all = [back[local_out]]
+        t = 1
+        while t < response:
+            k_now = back[(local_out + t) % response]
+            next_value = lax.ppermute(
+                k_now,
+                axis_name=lane_axis,
+                perm=[(pp, (pp + t) % response) for pp in range(response)],
+            )
+            xs_all.append(next_value)
+            t += 1
+        y_new = jnp.stack(xs_all, 0)
+        back = y_new[(local_out - jnp.arange(response)) % response]
+        return _treat_keys(back, slab_in)
+
+    arrived = read_sheet_on(x_slab, "expert", 0, 0)
     x_rows = arrived.reshape(row_total, feature_cols)
     gate_part = jnp.dot(x_rows, gate_mat, preferred_element_type=jnp.float32)
     up_part = jnp.dot(x_rows, up_mat, preferred_element_type=jnp.float32)

time: 263 us -> 283 us (1.076)
  starting transfers between devices: 23.7 us -> 54.6 us
  waiting for transfers between devices: 193 us -> 176 us
  local copies, waits for them, and re-layouts: 1.18 us -> 15.3 us
  matrix products: 39.4 us -> 32.6 us
    ppermute x0 -> x15, waiting for transfers between devices: none -> 68.5 us  [read_sheet_on(): lax.ppermute(k_now, axis_name=lane_axis, perm=[(pp, (pp + t) % response)...]
    all_to_all x1, waiting for transfers between devices: 39.9 us -> 0.01 us  [local(): lax.all_to_all(c_slab, 'expert', split_axis=0, concat_axis=0, tiled=True)]
    all_to_all x1 -> x0, waiting for transfers between devices: 37.5 us -> none  [local(): lax.all_to_all(x_slab, 'expert', split_axis=0, concat_axis=0, tiled=True)]
    ppermute x0 -> x15, starting transfers between devices: none -> 32.3 us  [read_sheet_on(): lax.ppermute(k_now, axis_name=lane_axis, perm=[(pp, (pp + t) % response)...]
    all_to_all x1, waiting for transfers between devices: 35.2 us -> 5.28 us  [local(): lax.all_to_all(out_rows, 'expert', split_axis=0, concat_axis=0, tiled=True)]
    ppermute x3, waiting for transfers between devices: 45.6 us -> 67.8 us  [dp_sum(): lax.ppermute(part, 'dp', [(i, (i + shift) % count) for i in range(count)])]
    unnamed x22 -> x46, local copies, waits for them, and re-layouts: 1.02 us -> 11.5 us
    all_to_all x1 -> x0, starting transfers between devices: 4.78 us -> none  [local(): lax.all_to_all(x_slab, 'expert', split_axis=0, concat_axis=0, tiled=True)]
  transfers between devices with their start and end apart: 7 -> 21, of which waited for: 6 -> 16; matrix products, arithmetic and copies ran while one was open for 11% -> 15% of each run, Pallas kernels for 0% -> 0%
where the time goes in v1:
time: 283 us
  waiting for transfers between devices  176 us (62%)
  starting transfers between devices  54.6 us (19%)
  matrix products  32.6 us (12%)
  local copies, waits for them, and re-layouts  15.3 us (5%)
  other arithmetic  2.86 us (1%)
    ppermute x15, waiting for transfers between devices, read_sheet_on(): lax.ppermute(k_now, axis_name=lane_axis, perm=[(pp, (pp + t) % response)...  68.5 us
    ppermute x3, waiting for transfers between devices, dp_sum(): lax.ppermute(part, 'dp', [(i, (i + shift) % count) for i in range(count)])  67.8 us
    all_to_all x1, waiting for transfers between devices, local(): lax.all_to_all(grad_rows, 'expert', split_axis=0, concat_axis=0, tiled=True)  34.8 us
    ppermute x15, starting transfers between devices, read_sheet_on(): lax.ppermute(k_now, axis_name=lane_axis, perm=[(pp, (pp + t) % response)...  32.3 us
    unnamed x46, local copies, waits for them, and re-layouts  11.5 us
    all_to_all x1, starting transfers between devices, local(): lax.all_to_all(out_rows, 'expert', split_axis=0, concat_axis=0, tiled=True)  9.08 us
    all_to_all x1, starting transfers between devices, local(): lax.all_to_all(c_slab, 'expert', split_axis=0, concat_axis=0, tiled=True)  6.65 us
  transfers between devices with their start and end apart: 21, of which 16 were waited for; matrix products, arithmetic and copies ran while one was open for 15% of the time, Pallas kernels for 0%

profile of v1, /device:TPU:15, one launch (start us, length us, event | category | flops | bytes accessed | tf_op | source)
XLA Modules:
  0.0 282.8 jit_solution(7573314023753940953)
XLA Ops:
  4.7 6.7 %all-to-all-start.1 = ((bf16[16,32,1792]{2,1,0:T(8,128)(2,1)}), bf16[16,32,1792]{2,1,0:T(8,128)(2,1)}, u32[]{:S(2)}, u32[]{:S(2)}) async-start(bf16[16,32,1792]{2,1,0:T(8,128)(2,1)} %bitcast.40), calls=%async_computation.1 | async-start | bytes 3670016 | tf_op jit(solution)/shard_map/all_to_all | solution.py:93
  15.1 3.2 %collective-permute-start.11 = (bf16[1,32,1792]{2,1,0:T(8,128)(2,1)S(1)}, bf16[1,32,1792]{2,1,0:T(8,128)(2,1)S(1)}, u32[]{:S(2)}, u32[]{:S(2)}) collective-permute-start(bf16[1,32,1792]{2,1,0:T(8,128)(2,1)S(1)} %get-tuple-element.6), channel_id=1, source_target_pairs={{0,12},{1,13},{2,14},{3,15},{4,0},{5,1},{6,2},{7,3},{8,4},{9,5},{1... | collective-permute-start | bytes 344072 | tf_op jit(solution)/shard_map/ppermute | solution.py:67
  19.6 36.8 %collective-permute-done = bf16[1,32,1792]{2,1,0:T(8,128)(2,1)S(1)} collective-permute-done((bf16[1,32,1792]{2,1,0:T(8,128)(2,1)S(1)}, bf16[1,32,1792]{2,1,0:T(8,128)(2,1)S(1)}, u32[]{:S(2)}, u32[]{:S(2)}) %collective-permute-start) | collective-permute-done | bytes 114720 | tf_op jit(solution)/shard_map/ppermute | solution.py:67
  57.0 3.0 %collective-permute-done.1 = bf16[1,32,1792]{2,1,0:T(8,128)(2,1)S(1)} collective-permute-done((bf16[1,32,1792]{2,1,0:T(8,128)(2,1)S(1)}, bf16[1,32,1792]{2,1,0:T(8,128)(2,1)S(1)}, u32[]{:S(2)}, u32[]{:S(2)}) %collective-permute-start.1) | collective-permute-done | bytes 114720 | tf_op jit(solution)/shard_map/ppermute | solution.py:67
  60.0 3.1 %collective-permute-start.2 = (bf16[1,32,1792]{2,1,0:T(8,128)(2,1)S(1)}, bf16[1,32,1792]{2,1,0:T(8,128)(2,1)S(1)}, u32[]{:S(2)}, u32[]{:S(2)}) collective-permute-start(bf16[1,32,1792]{2,1,0:T(8,128)(2,1)S(1)} %get-tuple-element.15), channel_id=1, source_target_pairs={{0,3},{1,4},{2,5},{3,6},{4,7},{5,8},{6,9},{7,10},{8,11},{9,12},{10... | collective-permute-start | bytes 344072 | tf_op jit(solution)/shard_map/ppermute | solution.py:67
  65.7 2.5 collective-permute-start.3
  70.7 3.2 %collective-permute-start.4 = (bf16[1,32,1792]{2,1,0:T(8,128)(2,1)S(1)}, bf16[1,32,1792]{2,1,0:T(8,128)(2,1)S(1)}, u32[]{:S(2)}, u32[]{:S(2)}) collective-permute-start(bf16[1,32,1792]{2,1,0:T(8,128)(2,1)S(1)} %get-tuple-element.13), channel_id=1, source_target_pairs={{0,5},{1,6},{2,7},{3,8},{4,9},{5,10},{6,11},{7,12},{8,13},{9,14},{... | collective-permute-start | bytes 344072 | tf_op jit(solution)/shard_map/ppermute | solution.py:67
  74.6 3.1 %collective-permute-done.4 = bf16[1,32,1792]{2,1,0:T(8,128)(2,1)S(1)} collective-permute-done((bf16[1,32,1792]{2,1,0:T(8,128)(2,1)S(1)}, bf16[1,32,1792]{2,1,0:T(8,128)(2,1)S(1)}, u32[]{:S(2)}, u32[]{:S(2)}) %collective-permute-start.4) | collective-permute-done | bytes 114720 | tf_op jit(solution)/shard_map/ppermute | solution.py:67
  82.2 3.0 %collective-permute-start.6 = (bf16[1,32,1792]{2,1,0:T(8,128)(2,1)S(1)}, bf16[1,32,1792]{2,1,0:T(8,128)(2,1)S(1)}, u32[]{:S(2)}, u32[]{:S(2)}) collective-permute-start(bf16[1,32,1792]{2,1,0:T(8,128)(2,1)S(1)} %get-tuple-element.11), channel_id=1, source_target_pairs={{0,7},{1,8},{2,9},{3,10},{4,11},{5,12},{6,13},{7,14},{8,15},{9,0},... | collective-permute-start | bytes 344072 | tf_op jit(solution)/shard_map/ppermute | solution.py:67
  85.9 5.2 %collective-permute-done.6 = bf16[1,32,1792]{2,1,0:T(8,128)(2,1)S(1)} collective-permute-done((bf16[1,32,1792]{2,1,0:T(8,128)(2,1)S(1)}, bf16[1,32,1792]{2,1,0:T(8,128)(2,1)S(1)}, u32[]{:S(2)}, u32[]{:S(2)}) %collective-permute-start.6) | collective-permute-done | bytes 114720 | tf_op jit(solution)/shard_map/ppermute | solution.py:67
  91.9 4.8 %collective-permute-done.7 = bf16[1,32,1792]{2,1,0:T(8,128)(2,1)S(1)} collective-permute-done((bf16[1,32,1792]{2,1,0:T(8,128)(2,1)S(1)}, bf16[1,32,1792]{2,1,0:T(8,128)(2,1)S(1)}, u32[]{:S(2)}, u32[]{:S(2)}) %collective-permute-start.7) | collective-permute-done | bytes 114720 | tf_op jit(solution)/shard_map/ppermute | solution.py:67
  96.6 5.1 %collective-permute-start.8 = (bf16[1,32,1792]{2,1,0:T(8,128)(2,1)S(1)}, bf16[1,32,1792]{2,1,0:T(8,128)(2,1)S(1)}, u32[]{:S(2)}, u32[]{:S(2)}) collective-permute-start(bf16[1,32,1792]{2,1,0:T(8,128)(2,1)S(1)} %get-tuple-element.9), channel_id=1, source_target_pairs={{0,9},{1,10},{2,11},{3,12},{4,13},{5,14},{6,15},{7,0},{8,1},{9,2},... | collective-permute-start | bytes 344072 | tf_op jit(solution)/shard_map/ppermute | solution.py:67
  102.3 2.3 collective-permute-done.8
  104.6 3.5 %collective-permute-start.9 = (bf16[1,32,1792]{2,1,0:T(8,128)(2,1)S(1)}, bf16[1,32,1792]{2,1,0:T(8,128)(2,1)S(1)}, u32[]{:S(2)}, u32[]{:S(2)}) collective-permute-start(bf16[1,32,1792]{2,1,0:T(8,128)(2,1)S(1)} %get-tuple-element.8), channel_id=1, source_target_pairs={{0,10},{1,11},{2,12},{3,13},{4,14},{5,15},{6,0},{7,1},{8,2},{9,3},... | collective-permute-start | bytes 344072 | tf_op jit(solution)/shard_map/ppermute | solution.py:67
  108.8 4.1 %collective-permute-done.9 = bf16[1,32,1792]{2,1,0:T(8,128)(2,1)S(1)} collective-permute-done((bf16[1,32,1792]{2,1,0:T(8,128)(2,1)S(1)}, bf16[1,32,1792]{2,1,0:T(8,128)(2,1)S(1)}, u32[]{:S(2)}, u32[]{:S(2)}) %collective-permute-start.9) | collective-permute-done | bytes 114720 | tf_op jit(solution)/shard_map/ppermute | solution.py:67
  112.8 3.3 %collective-permute-start.10 = (bf16[1,32,1792]{2,1,0:T(8,128)(2,1)S(1)}, bf16[1,32,1792]{2,1,0:T(8,128)(2,1)S(1)}, u32[]{:S(2)}, u32[]{:S(2)}) collective-permute-start(bf16[1,32,1792]{2,1,0:T(8,128)(2,1)S(1)} %get-tuple-element.7), channel_id=1, source_target_pairs={{0,11},{1,12},{2,13},{3,14},{4,15},{5,0},{6,1},{7,2},{8,3},{9,4},{... | collective-permute-start | bytes 344072 | tf_op jit(solution)/shard_map/ppermute | solution.py:67
  116.8 3.5 %collective-permute-done.10 = bf16[1,32,1792]{2,1,0:T(8,128)(2,1)S(1)} collective-permute-done((bf16[1,32,1792]{2,1,0:T(8,128)(2,1)S(1)}, bf16[1,32,1792]{2,1,0:T(8,128)(2,1)S(1)}, u32[]{:S(2)}, u32[]{:S(2)}) %collective-permute-start.10) | collective-permute-done | bytes 114720 | tf_op jit(solution)/shard_map/ppermute | solution.py:67
  123.6 2.2 gather_fusion
  125.8 4.2 %fusion.22 = bf16[512,1024]{1,0:T(8,128)(2,1)S(1)} fusion(bf16[512,1792]{1,0:T(8,128)(2,1)S(1)} %bitcast.121, bf16[1,1792,1024]{2,1,0:T(8,128)(2,1)} %param.10), kind=kOutput, calls=%fused_computation.33 | convolution fusion | flops 1879572480 | bytes 6553600 | tf_op jit(solution)/shard_map/dot_general | solution.py:80
  130.1 2.1 fusion.25
  133.7 23.7 %collective-permute-done.16 = bf16[512,1024]{1,0:T(8,128)(2,1)S(1)} collective-permute-done((bf16[512,1024]{1,0:T(8,128)(2,1)S(1)}, bf16[512,1024]{1,0:T(8,128)(2,1)S(1)}, u32[]{:S(2)}, u32[]{:S(2)}) %collective-permute-start.16) | collective-permute-done | bytes 1048608 | tf_op jit(solution)/shard_map/ppermute | solution.py:24
  157.4 20.0 %collective-permute-done.15 = bf16[512,1024]{1,0:T(8,128)(2,1)S(1)} collective-permute-done((bf16[512,1024]{1,0:T(8,128)(2,1)S(1)}, bf16[512,1024]{1,0:T(8,128)(2,1)S(1)}, u32[]{:S(2)}, u32[]{:S(2)}) %collective-permute-start.15) | collective-permute-done | bytes 1048608 | tf_op jit(solution)/shard_map/ppermute | solution.py:24
  179.5 3.3 %fusion.15 = bf16[512,1792]{1,0:T(8,128)(2,1)} fusion(bf16[512,1024]{1,0:T(8,128)(2,1)S(1)} %multiply_convert_fusion.4, bf16[1,1024,1792]{2,1,0:T(8,128)(2,1)S(1)} %copy-done.12), kind=kOutput, calls=%fused_computation.18 | convolution fusion | flops 1879965696 | bytes 6553600 | tf_op jit(solution)/shard_map/dot_general | solution.py:85
  182.8 9.1 %all-to-all-start = ((bf16[16,32,1792]{2,1,0:T(8,128)(2,1)}), bf16[16,32,1792]{2,1,0:T(8,128)(2,1)S(1)}, u32[]{:S(2)}, u32[]{:S(2)}) async-start(bf16[16,32,1792]{2,1,0:T(8,128)(2,1)} %bitcast.119), calls=%async_computation | async-start | bytes 3670016 | tf_op jit(solution)/shard_map/all_to_all | solution.py:92
  191.9 4.8 %fusion.28 = bf16[512,1024]{1,0:T(8,128)(2,1)S(1)} fusion(bf16[512,1792]{1,0:T(8,128)(2,1)} %bitcast.41, bf16[1,1024,1792]{2,1,0:T(8,128)(2,1)} %param.12), kind=kOutput, calls=%fused_computation.35 | convolution fusion | flops 1879572480 | bytes 6553600 | tf_op jit(solution)/shard_map/dot_general | solution.py:95
  197.1 24.1 %collective-permute-done.17 = bf16[512,1024]{1,0:T(8,128)(2,1)S(1)} collective-permute-done((bf16[512,1024]{1,0:T(8,128)(2,1)S(1)}, bf16[512,1024]{1,0:T(8,128)(2,1)S(1)}, u32[]{:S(2)}, u32[]{:S(2)}) %collective-permute-start.17) | collective-permute-done | bytes 1048608 | tf_op jit(solution)/shard_map/ppermute | solution.py:24
  221.2 3.2 %fusion.8 = f32[512,1792]{1,0:T(8,128)S(1)} fusion(bf16[1,1792,1024]{2,1,0:T(8,128)(2,1)S(1)} %copy-done.13, bf16[512,1024]{1,0:T(8,128)(2,1)S(1)} %copy-done.10, bf16[512,1024]{1,0:T(8,128)(2,1)S(1)} %fusion.22, bf16[512,1024]{1,0:T(8,128)(2,1)S(1)} %copy-done.8, bf16[512,1024]{1,0:T(8,128)(2,1)S(1)} %copy-done.6, ...), kind=kOutput, calls=%fused_computation.10 | convolution fusion | flops 1889009664 | bytes 13631488 | tf_op jit(solution)/shard_map/dot_general | solution.py:100
  224.4 4.0 %add_convert_fusion = bf16[512,1792]{1,0:T(8,128)(2,1)} fusion(f32[512,1792]{1,0:T(8,128)S(1)} %fusion.8, bf16[1,1792,1024]{2,1,0:T(8,128)(2,1)S(1)} %copy-done.15, bf16[512,1024]{1,0:T(8,128)(2,1)S(1)} %collective-permute-done.17, bf16[512,1024]{1,0:T(8,128)(2,1)S(1)} %fusion.28, bf16[512,1024]{1,0:T(8,128)(2,1)S(1)} %copy-done.10, ...), kind=kOutput, calls=%fused_computation.14 | convolution fusion | flops 1887174656 | bytes 13369344 | tf_op jit(solution)/shard_map/dot_general | solution.py:101
  228.4 5.3 %all-to-all-done = bf16[16,32,1792]{2,1,0:T(8,128)(2,1)S(1)} async-done(((bf16[16,32,1792]{2,1,0:T(8,128)(2,1)}), bf16[16,32,1792]{2,1,0:T(8,128)(2,1)S(1)}, u32[]{:S(2)}, u32[]{:S(2)}) %all-to-all-start) | async-done | bytes 1835040 | tf_op jit(solution)/shard_map/all_to_all | solution.py:92
  235.0 4.8 %all-to-all-start.2 = ((bf16[16,32,1792]{2,1,0:T(8,128)(2,1)}), bf16[16,32,1792]{2,1,0:T(8,128)(2,1)S(1)}, u32[]{:S(2)}, u32[]{:S(2)}) async-start(bf16[16,32,1792]{2,1,0:T(8,128)(2,1)} %bitcast.120), calls=%async_computation.2 | async-start | bytes 3670016 | tf_op jit(solution)/shard_map/all_to_all | solution.py:109
  239.8 5.6 %fusion.12 = bf16[1,1024,1792]{2,1,0:T(8,128)(2,1)} fusion(bf16[512,1024]{1,0:T(8,128)(2,1)S(1)} %copy-done.4, bf16[512,1792]{1,0:T(8,128)(2,1)} %bitcast.41), kind=kOutput, calls=%fused_computation.17 | convolution fusion | flops 1880883200 | bytes 6553600 | tf_op jit(solution)/shard_map/dot_general | solution.py:105
  246.7 34.8 %all-to-all-done.2 = bf16[16,32,1792]{2,1,0:T(8,128)(2,1)S(1)} async-done(((bf16[16,32,1792]{2,1,0:T(8,128)(2,1)}), bf16[16,32,1792]{2,1,0:T(8,128)(2,1)S(1)}, u32[]{:S(2)}, u32[]{:S(2)}) %all-to-all-start.2) | async-done | bytes 1835040 | tf_op jit(solution)/shard_map/all_to_all | solution.py:109
  (81 shorter events, 34.3 us)
Async XLA Ops:
  4.7 6.7 %copy-start.11 = (bf16[128,1792]{1,0:T(8,128)(2,1)S(1)}, bf16[128,1792]{1,0:T(8,128)(2,1)}, u32[]{:S(2)}) copy-start(bf16[128,1792]{1,0:T(8,128)(2,1)} %param.7) | copy-start | bytes 1376260
  4.7 178.1 %all-to-all-start.1 = ((bf16[16,32,1792]{2,1,0:T(8,128)(2,1)}), bf16[16,32,1792]{2,1,0:T(8,128)(2,1)}, u32[]{:S(2)}, u32[]{:S(2)}) async-start(bf16[16,32,1792]{2,1,0:T(8,128)(2,1)} %bitcast.40), calls=%async_computation.1 | async-start | bytes 3670016 | tf_op jit(solution)/shard_map/all_to_all | solution.py:93
  12.9 110.0 %collective-permute-start.14 = (bf16[1,32,1792]{2,1,0:T(8,128)(2,1)S(1)}, bf16[1,32,1792]{2,1,0:T(8,128)(2,1)S(1)}, u32[]{:S(2)}, u32[]{:S(2)}) collective-permute-start(bf16[1,32,1792]{2,1,0:T(8,128)(2,1)S(1)} %get-tuple-element.3), channel_id=1, source_target_pairs={{0,15},{1,0},{2,1},{3,2},{4,3},{5,4},{6,5},{7,6},{8,7},{9,8},{10,9... | collective-permute-start | bytes 344072 | tf_op jit(solution)/shard_map/ppermute | solution.py:67
  13.3 108.9 %collective-permute-start.13 = (bf16[1,32,1792]{2,1,0:T(8,128)(2,1)S(1)}, bf16[1,32,1792]{2,1,0:T(8,128)(2,1)S(1)}, u32[]{:S(2)}, u32[]{:S(2)}) collective-permute-start(bf16[1,32,1792]{2,1,0:T(8,128)(2,1)S(1)} %get-tuple-element.4), channel_id=1, source_target_pairs={{0,14},{1,15},{2,0},{3,1},{4,2},{5,3},{6,4},{7,5},{8,6},{9,7},{10,... | collective-permute-start | bytes 344072 | tf_op jit(solution)/shard_map/ppermute | solution.py:67
  13.6 108.0 %collective-permute-start.12 = (bf16[1,32,1792]{2,1,0:T(8,128)(2,1)S(1)}, bf16[1,32,1792]{2,1,0:T(8,128)(2,1)S(1)}, u32[]{:S(2)}, u32[]{:S(2)}) collective-permute-start(bf16[1,32,1792]{2,1,0:T(8,128)(2,1)S(1)} %get-tuple-element.5), channel_id=1, source_target_pairs={{0,13},{1,14},{2,15},{3,0},{4,1},{5,2},{6,3},{7,4},{8,5},{9,6},{10... | collective-permute-start | bytes 344072 | tf_op jit(solution)/shard_map/ppermute | solution.py:67
  15.1 105.9 %collective-permute-start.11 = (bf16[1,32,1792]{2,1,0:T(8,128)(2,1)S(1)}, bf16[1,32,1792]{2,1,0:T(8,128)(2,1)S(1)}, u32[]{:S(2)}, u32[]{:S(2)}) collective-permute-start(bf16[1,32,1792]{2,1,0:T(8,128)(2,1)S(1)} %get-tuple-element.6), channel_id=1, source_target_pairs={{0,12},{1,13},{2,14},{3,15},{4,0},{5,1},{6,2},{7,3},{8,4},{9,5},{1... | collective-permute-start | bytes 344072 | tf_op jit(solution)/shard_map/ppermute | solution.py:67
  18.2 38.1 %collective-permute-start = (bf16[1,32,1792]{2,1,0:T(8,128)(2,1)S(1)}, bf16[1,32,1792]{2,1,0:T(8,128)(2,1)S(1)}, u32[]{:S(2)}, u32[]{:S(2)}) collective-permute-start(bf16[1,32,1792]{2,1,0:T(8,128)(2,1)S(1)} %get-tuple-element.17), channel_id=1, source_target_pairs={{0,1},{1,2},{2,3},{3,4},{4,5},{5,6},{6,7},{7,8},{8,9},{9,10},{10,1... | collective-permute-start | bytes 344072 | tf_op jit(solution)/shard_map/ppermute | solution.py:67
  56.4 3.6 %collective-permute-start.1 = (bf16[1,32,1792]{2,1,0:T(8,128)(2,1)S(1)}, bf16[1,32,1792]{2,1,0:T(8,128)(2,1)S(1)}, u32[]{:S(2)}, u32[]{:S(2)}) collective-permute-start(bf16[1,32,1792]{2,1,0:T(8,128)(2,1)S(1)} %get-tuple-element.16), channel_id=1, source_target_pairs={{0,2},{1,3},{2,4},{3,5},{4,6},{5,7},{6,8},{7,9},{8,10},{9,11},{10,... | collective-permute-start | bytes 344072 | tf_op jit(solution)/shard_map/ppermute | solution.py:67
  60.0 5.6 %collective-permute-start.2 = (bf16[1,32,1792]{2,1,0:T(8,128)(2,1)S(1)}, bf16[1,32,1792]{2,1,0:T(8,128)(2,1)S(1)}, u32[]{:S(2)}, u32[]{:S(2)}) collective-permute-start(bf16[1,32,1792]{2,1,0:T(8,128)(2,1)S(1)} %get-tuple-element.15), channel_id=1, source_target_pairs={{0,3},{1,4},{2,5},{3,6},{4,7},{5,8},{6,9},{7,10},{8,11},{9,12},{10... | collective-permute-start | bytes 344072 | tf_op jit(solution)/shard_map/ppermute | solution.py:67
  65.7 5.0 %collective-permute-start.3 = (bf16[1,32,1792]{2,1,0:T(8,128)(2,1)S(1)}, bf16[1,32,1792]{2,1,0:T(8,128)(2,1)S(1)}, u32[]{:S(2)}, u32[]{:S(2)}) collective-permute-start(bf16[1,32,1792]{2,1,0:T(8,128)(2,1)S(1)} %get-tuple-element.14), channel_id=1, source_target_pairs={{0,4},{1,5},{2,6},{3,7},{4,8},{5,9},{6,10},{7,11},{8,12},{9,13},{1... | collective-permute-start | bytes 344072 | tf_op jit(solution)/shard_map/ppermute | solution.py:67
  70.7 7.0 %collective-permute-start.4 = (bf16[1,32,1792]{2,1,0:T(8,128)(2,1)S(1)}, bf16[1,32,1792]{2,1,0:T(8,128)(2,1)S(1)}, u32[]{:S(2)}, u32[]{:S(2)}) collective-permute-start(bf16[1,32,1792]{2,1,0:T(8,128)(2,1)S(1)} %get-tuple-element.13), channel_id=1, source_target_pairs={{0,5},{1,6},{2,7},{3,8},{4,9},{5,10},{6,11},{7,12},{8,13},{9,14},{... | collective-permute-start | bytes 344072 | tf_op jit(solution)/shard_map/ppermute | solution.py:67
  77.6 4.5 %collective-permute-start.5 = (bf16[1,32,1792]{2,1,0:T(8,128)(2,1)S(1)}, bf16[1,32,1792]{2,1,0:T(8,128)(2,1)S(1)}, u32[]{:S(2)}, u32[]{:S(2)}) collective-permute-start(bf16[1,32,1792]{2,1,0:T(8,128)(2,1)S(1)} %get-tuple-element.12), channel_id=1, source_target_pairs={{0,6},{1,7},{2,8},{3,9},{4,10},{5,11},{6,12},{7,13},{8,14},{9,15},... | collective-permute-start | bytes 344072 | tf_op jit(solution)/shard_map/ppermute | solution.py:67
  82.2 8.9 %collective-permute-start.6 = (bf16[1,32,1792]{2,1,0:T(8,128)(2,1)S(1)}, bf16[1,32,1792]{2,1,0:T(8,128)(2,1)S(1)}, u32[]{:S(2)}, u32[]{:S(2)}) collective-permute-start(bf16[1,32,1792]{2,1,0:T(8,128)(2,1)S(1)} %get-tuple-element.11), channel_id=1, source_target_pairs={{0,7},{1,8},{2,9},{3,10},{4,11},{5,12},{6,13},{7,14},{8,15},{9,0},... | collective-permute-start | bytes 344072 | tf_op jit(solution)/shard_map/ppermute | solution.py:67
  91.1 5.6 %collective-permute-start.7 = (bf16[1,32,1792]{2,1,0:T(8,128)(2,1)S(1)}, bf16[1,32,1792]{2,1,0:T(8,128)(2,1)S(1)}, u32[]{:S(2)}, u32[]{:S(2)}) collective-permute-start(bf16[1,32,1792]{2,1,0:T(8,128)(2,1)S(1)} %get-tuple-element.10), channel_id=1, source_target_pairs={{0,8},{1,9},{2,10},{3,11},{4,12},{5,13},{6,14},{7,15},{8,0},{9,1},... | collective-permute-start | bytes 344072 | tf_op jit(solution)/shard_map/ppermute | solution.py:67
  96.6 8.0 %collective-permute-start.8 = (bf16[1,32,1792]{2,1,0:T(8,128)(2,1)S(1)}, bf16[1,32,1792]{2,1,0:T(8,128)(2,1)S(1)}, u32[]{:S(2)}, u32[]{:S(2)}) collective-permute-start(bf16[1,32,1792]{2,1,0:T(8,128)(2,1)S(1)} %get-tuple-element.9), channel_id=1, source_target_pairs={{0,9},{1,10},{2,11},{3,12},{4,13},{5,14},{6,15},{7,0},{8,1},{9,2},... | collective-permute-start | bytes 344072 | tf_op jit(solution)/shard_map/ppermute | solution.py:67
  104.6 8.2 %collective-permute-start.9 = (bf16[1,32,1792]{2,1,0:T(8,128)(2,1)S(1)}, bf16[1,32,1792]{2,1,0:T(8,128)(2,1)S(1)}, u32[]{:S(2)}, u32[]{:S(2)}) collective-permute-start(bf16[1,32,1792]{2,1,0:T(8,128)(2,1)S(1)} %get-tuple-element.8), channel_id=1, source_target_pairs={{0,10},{1,11},{2,12},{3,13},{4,14},{5,15},{6,0},{7,1},{8,2},{9,3},... | collective-permute-start | bytes 344072 | tf_op jit(solution)/shard_map/ppermute | solution.py:67
  112.8 7.5 %collective-permute-start.10 = (bf16[1,32,1792]{2,1,0:T(8,128)(2,1)S(1)}, bf16[1,32,1792]{2,1,0:T(8,128)(2,1)S(1)}, u32[]{:S(2)}, u32[]{:S(2)}) collective-permute-start(bf16[1,32,1792]{2,1,0:T(8,128)(2,1)S(1)} %get-tuple-element.7), channel_id=1, source_target_pairs={{0,11},{1,12},{2,13},{3,14},{4,15},{5,0},{6,1},{7,2},{8,3},{9,4},{... | collective-permute-start | bytes 344072 | tf_op jit(solution)/shard_map/ppermute | solution.py:67
  132.2 46.3 %copy-start.5 = (bf16[512,1024]{1,0:T(8,128)(2,1)}, bf16[512,1024]{1,0:T(8,128)(2,1)S(1)}, u32[]{:S(2)}) copy-start(bf16[512,1024]{1,0:T(8,128)(2,1)S(1)} %fusion.25) | copy-start | bytes 3145732
  132.2 47.3 %copy-start.12 = (bf16[1,1024,1792]{2,1,0:T(8,128)(2,1)S(1)}, bf16[1,1024,1792]{2,1,0:T(8,128)(2,1)}, u32[]{:S(2)}) copy-start(bf16[1,1024,1792]{2,1,0:T(8,128)(2,1)} %param.12) | copy-start | bytes 11010052
  132.2 25.2 %collective-permute-start.16 = (bf16[512,1024]{1,0:T(8,128)(2,1)S(1)}, bf16[512,1024]{1,0:T(8,128)(2,1)S(1)}, u32[]{:S(2)}, u32[]{:S(2)}) collective-permute-start(bf16[512,1024]{1,0:T(8,128)(2,1)S(1)} %fusion.25), channel_id=1, source_target_pairs={{0,16},{16,0},{1,17},{17,1},{2,18},{18,2},{3,19},{19,3},{4,20},{20... | collective-permute-start | bytes 3145736 | tf_op jit(solution)/shard_map/ppermute | solution.py:24
  132.5 44.9 %collective-permute-start.15 = (bf16[512,1024]{1,0:T(8,128)(2,1)S(1)}, bf16[512,1024]{1,0:T(8,128)(2,1)S(1)}, u32[]{:S(2)}, u32[]{:S(2)}) collective-permute-start(bf16[512,1024]{1,0:T(8,128)(2,1)S(1)} %fusion.22), channel_id=1, source_target_pairs={{0,16},{16,0},{1,17},{17,1},{2,18},{18,2},{3,19},{19,3},{4,20},{20... | collective-permute-start | bytes 3145736 | tf_op jit(solution)/shard_map/ppermute | solution.py:24
  157.4 21.1 %copy-start.7 = (bf16[512,1024]{1,0:T(8,128)(2,1)}, bf16[512,1024]{1,0:T(8,128)(2,1)S(1)}, u32[]{:S(2)}) copy-start(bf16[512,1024]{1,0:T(8,128)(2,1)S(1)} %collective-permute-done.16) | copy-start | bytes 3145732
  182.8 50.9 %all-to-all-start = ((bf16[16,32,1792]{2,1,0:T(8,128)(2,1)}), bf16[16,32,1792]{2,1,0:T(8,128)(2,1)S(1)}, u32[]{:S(2)}, u32[]{:S(2)}) async-start(bf16[16,32,1792]{2,1,0:T(8,128)(2,1)} %bitcast.119), calls=%async_computation | async-start | bytes 3670016 | tf_op jit(solution)/shard_map/all_to_all | solution.py:92
  191.9 29.3 %copy-start.6 = (bf16[512,1024]{1,0:T(8,128)(2,1)S(1)}, bf16[512,1024]{1,0:T(8,128)(2,1)}, u32[]{:S(2)}) copy-start(bf16[512,1024]{1,0:T(8,128)(2,1)} %copy-done.5) | copy-start | bytes 3145732
  191.9 29.3 %copy-start.8 = (bf16[512,1024]{1,0:T(8,128)(2,1)S(1)}, bf16[512,1024]{1,0:T(8,128)(2,1)}, u32[]{:S(2)}) copy-start(bf16[512,1024]{1,0:T(8,128)(2,1)} %copy-done.7) | copy-start | bytes 3145732
  191.9 29.3 %copy-start.10 = (bf16[512,1024]{1,0:T(8,128)(2,1)S(1)}, bf16[512,1024]{1,0:T(8,128)(2,1)}, u32[]{:S(2)}) copy-start(bf16[512,1024]{1,0:T(8,128)(2,1)} %copy-done.9) | copy-start | bytes 3145732
  191.9 29.3 %copy-start.13 = (bf16[1,1792,1024]{2,1,0:T(8,128)(2,1)S(1)}, bf16[1,1792,1024]{2,1,0:T(8,128)(2,1)}, u32[]{:S(2)}) copy-start(bf16[1,1792,1024]{2,1,0:T(8,128)(2,1)} %param.10) | copy-start | bytes 11010052
  196.8 27.6 %copy-start.15 = (bf16[1,1792,1024]{2,1,0:T(8,128)(2,1)S(1)}, bf16[1,1792,1024]{2,1,0:T(8,128)(2,1)}, u32[]{:S(2)}) copy-start(bf16[1,1792,1024]{2,1,0:T(8,128)(2,1)} %param.11) | copy-start | bytes 11010052
  196.8 24.4 %collective-permute-start.17 = (bf16[512,1024]{1,0:T(8,128)(2,1)S(1)}, bf16[512,1024]{1,0:T(8,128)(2,1)S(1)}, u32[]{:S(2)}, u32[]{:S(2)}) collective-permute-start(bf16[512,1024]{1,0:T(8,128)(2,1)S(1)} %fusion.28), channel_id=1, source_target_pairs={{0,16},{16,0},{1,17},{17,1},{2,18},{18,2},{3,19},{19,3},{4,20},{20... | collective-permute-start | bytes 3145736 | tf_op jit(solution)/shard_map/ppermute | solution.py:24
  228.4 11.3 %copy-start.4 = (bf16[512,1024]{1,0:T(8,128)(2,1)S(1)}, bf16[512,1024]{1,0:T(8,128)(2,1)}, u32[]{:S(2)}) copy-start(bf16[512,1024]{1,0:T(8,128)(2,1)} %copy-done.3) | copy-start | bytes 3145732
  235.0 46.6 %all-to-all-start.2 = ((bf16[16,32,1792]{2,1,0:T(8,128)(2,1)}), bf16[16,32,1792]{2,1,0:T(8,128)(2,1)S(1)}, u32[]{:S(2)}, u32[]{:S(2)}) async-start(bf16[16,32,1792]{2,1,0:T(8,128)(2,1)} %bitcast.120), calls=%async_computation.2 | async-start | bytes 3670016 | tf_op jit(solution)/shard_map/all_to_all | solution.py:109
  239.7 5.6 %copy-start.2 = (bf16[16,32,1792]{2,1,0:T(8,128)(2,1)S(1)}, bf16[16,32,1792]{2,1,0:T(8,128)(2,1)}, u32[]{:S(2)}) copy-start(bf16[16,32,1792]{2,1,0:T(8,128)(2,1)} %copy-done.1) | copy-start | bytes 5505028
  (5 other events, 9.7 us)
